TPU v7x, 256 devices: a whole 4x4x8 slice. The times are simulated.
256 devices in a mesh: row: 16 (over z_lo, x, core), col: 4 (over y), item: 4 (over z_hi).
Axes of the slice: x: 4, y: 4, z: 8 (z_hi: 4, z_lo: 2; z = z_hi * 2 + z_lo), core: 2. Of those that a mesh axis runs over, the one named last changes fastest.
Arguments:
- tokens: bfloat16 [4, 16, 64, 2432], P('item', 'row', 'col'), may hold values from -6 to 6
- text_keys_values: bfloat16 [4, 154, 2, 2048], P('item', None, None, 'row'), may hold values from -200 to 200
- text_length: int32 [4], P('item'), may hold values from 2 to 154, as said below
- modulation: float32 [4, 8, 2432], P('item'), may hold values from -4 to 4
- input_weight: bfloat16 [2432, 3, 2048], P(None, None, 'row'), may hold values from -0.125 to 0.125
- norm_gain: float32 [2, 64], replicated, may hold values from 1 to 3
- output_weight: bfloat16 [2048, 2432], P('row'), may hold values from -0.125 to 0.125
- up_weight: bfloat16 [2432, 9728], P(None, 'row'), may hold values from -0.125 to 0.125
- down_weight: bfloat16 [9728, 2432], P('row'), may hold values from -0.0625 to 0.0625
- final_weight: bfloat16 [2432, 64], replicated, may hold values from -0.125 to 0.125
- step_index: int32 [1], replicated, may hold values from 0 to 27
- latent: float32 [4, 16, 4096], P('item', 'row', 'col'), may hold values from -6 to 6
Outputs:
- tokens_out: bfloat16 [4, 16, 64, 2432], P('item', 'row', 'col')
- velocity: float32 [4, 16, 4096], P('item', 'row', 'col')
- latent_next: float32 [4, 16, 4096], P('item', 'row', 'col')
Inputs may be any that keep to these rules, and one draw needn't show every extreme that they name: `text_length`: at least one sequence has all 154 text tokens valid.
All inputs are finite; a program needn't handle non-finite values.
Results may differ from a plain program's by a relative error of at most 0.024.
Values may be sent and summed in bfloat16 or wider, within the bound.
A program may use at most 64 MiB of HBM per device.

v0:
```python
import jax
import jax.numpy as jnp
from jax import lax
from jax.sharding import PartitionSpec as P

HD = 64
STEPS = 28
EPSILON = 1e-06
SHIFT_FACTOR = 3.0
GUIDANCE = 4.5
MASKED = -1e30


def partner_2(value, axis, apart):
    mask = 2**apart
    pairs = [(source, source ^ mask) for source in range(lax.axis_size(axis))]
    return lax.ppermute(value, axis, pairs)


def layer_norm(values):
    center = values - jnp.mean(values, axis=-1, keepdims=True)
    spread = jnp.mean(center * center, axis=-1, keepdims=True)
    return center * lax.rsqrt(spread + EPSILON)


def modulate(values, shift_term, scale_term):
    return (layer_norm(values) * (1.0 + scale_term) + shift_term).astype(jnp.bfloat16)


def root_norm(values, gain_row):
    return (
        values * lax.rsqrt(jnp.mean(values * values, axis=-1, keepdims=True) + EPSILON) * gain_row
    )


def noise_level(position):
    linear = 1.0 - position / STEPS
    return SHIFT_FACTOR * linear / (1.0 + (SHIFT_FACTOR - 1.0) * linear)


def on_device(
    tokens,
    text_keys_values,
    text_length,
    modulation,
    input_weight,
    norm_gain,
    output_weight,
    up_weight,
    down_weight,
    final_weight,
    step_index,
    latent,
):
    tile_rows = tokens.shape[1] * tokens.shape[2]
    model_width = tokens.shape[3]
    mod_rows = modulation[0]
    row_position = lax.axis_index("row")
    stripe_tokens = lax.all_gather(tokens, "row", axis=1, tiled=True)
    stripe_states = stripe_tokens.reshape(-1, model_width).astype(jnp.float32)
    stripe_rows = stripe_states.shape[0]
    local_width = input_weight.shape[2]
    local_heads = local_width // HD
    attn_input = modulate(stripe_states, mod_rows[0], mod_rows[1])
    projected = jnp.dot(
        attn_input,
        input_weight.reshape(model_width, 3 * local_width),
        preferred_element_type=jnp.float32,
    )
    projected = projected.reshape(stripe_rows, 3, local_heads, HD)
    queries = root_norm(projected[:, 0], norm_gain[0]).astype(jnp.bfloat16).transpose(1, 0, 2)
    keys_image = (
        root_norm(projected[:, 1], norm_gain[1])
        .astype(jnp.bfloat16)
        .reshape(stripe_rows, local_width)
    )
    values_image = projected[:, 2].astype(jnp.bfloat16).reshape(stripe_rows, local_width)
    text_pairs = text_keys_values[0]
    keys_text = text_pairs[:, 0].reshape(-1, local_heads, HD)
    values_text = text_pairs[:, 1].reshape(-1, local_heads, HD)
    text_valid = jnp.arange(keys_text.shape[0]) < text_length[0]
    text_scores = jnp.einsum(
        "hsd,thd->hst", queries, keys_text, preferred_element_type=jnp.float32
    ) * HD ** (-0.5)
    text_scores = jnp.where(text_valid[None, None, :], text_scores, MASKED)
    largest = jnp.max(text_scores, axis=-1)
    text_weights = jnp.exp(text_scores - largest[..., None])
    total_mass = jnp.sum(text_weights, axis=-1)
    weighted = jnp.einsum(
        "hst,thd->hsd",
        text_weights.astype(jnp.bfloat16),
        values_text,
        preferred_element_type=jnp.float32,
    )

    def one_block(running, block_pair):
        running_max, running_mass, running_sum = running
        key_block, value_block = block_pair
        scores = jnp.einsum(
            "hsd,khd->hsk", queries, key_block, preferred_element_type=jnp.float32
        ) * HD ** (-0.5)
        new_max = jnp.maximum(running_max, jnp.max(scores, axis=-1))
        factor = jnp.exp(running_max - new_max)
        weights = jnp.exp(scores - new_max[..., None])
        new_mass = running_mass * factor + jnp.sum(weights, axis=-1)
        new_sum = running_sum * factor[..., None] + jnp.einsum(
            "hsk,khd->hsd",
            weights.astype(jnp.bfloat16),
            value_block,
            preferred_element_type=jnp.float32,
        )
        return ((new_max, new_mass, new_sum), None)

    key_piece = lax.all_gather(keys_image, "col", axis=0, tiled=True)
    value_piece = lax.all_gather(values_image, "col", axis=0, tiled=True)
    blocks = key_piece.shape[0] // stripe_rows
    key_blocks = key_piece.reshape(blocks, stripe_rows, local_heads, HD)
    value_blocks = value_piece.reshape(blocks, stripe_rows, local_heads, HD)
    result, unused = lax.scan(
        one_block, (largest, total_mass, weighted), (key_blocks, value_blocks)
    )
    largest, total_mass, weighted = result
    attended = (
        (weighted / total_mass[..., None])
        .astype(jnp.bfloat16)
        .transpose(1, 0, 2)
        .reshape(stripe_rows, local_width)
    )
    attention = lax.psum(
        jnp.dot(attended, output_weight, preferred_element_type=jnp.float32).astype(jnp.bfloat16),
        "row",
    ).astype(jnp.float32)
    stripe_middle = stripe_states + mod_rows[2] * attention
    feed_input = modulate(stripe_middle, mod_rows[3], mod_rows[4])
    hidden = jax.nn.gelu(
        jnp.dot(feed_input, up_weight, preferred_element_type=jnp.float32), approximate=True
    ).astype(jnp.bfloat16)
    middle = lax.dynamic_slice_in_dim(stripe_middle, row_position * tile_rows, tile_rows, 0)
    feed = lax.psum_scatter(
        jnp.dot(hidden, down_weight, preferred_element_type=jnp.float32).astype(jnp.bfloat16),
        "row",
        scatter_dimension=0,
        tiled=True,
    ).astype(jnp.float32)
    leaving = middle + mod_rows[5] * feed
    tokens_out = leaving.astype(jnp.bfloat16).reshape(tokens.shape)
    final_input = modulate(leaving, mod_rows[6], mod_rows[7])
    raw_velocity = jnp.dot(final_input, final_weight, preferred_element_type=jnp.float32).reshape(
        1, tokens.shape[1], -1
    )
    partner = partner_2(raw_velocity, "item", 0)
    is_guided = lax.axis_index("item") % 2 == 0
    guided = jnp.where(is_guided, raw_velocity, partner)
    unguided = jnp.where(is_guided, partner, raw_velocity)
    velocity = unguided + GUIDANCE * (guided - unguided)
    position = step_index[0].astype(jnp.float32)
    step_size = noise_level(position + 1.0) - noise_level(position)
    return (tokens_out, velocity, latent + step_size * velocity)


def solution(mesh):
    in_specs = (
        P("item", "row", "col", None),
        P("item", None, None, "row"),
        P("item"),
        P("item", None, None),
        P(None, None, "row"),
        P(),
        P("row", None),
        P(None, "row"),
        P("row", None),
        P(),
        P(),
        P("item", "row", "col"),
    )
    out_specs = (P("item", "row", "col", None), P("item", "row", "col"), P("item", "row", "col"))
    return jax.shard_map(
        on_device, mesh=mesh, in_specs=in_specs, out_specs=out_specs, check_vma=False
    )
```

profile of v0, /device:TPU:8, one launch (start us, length us, event | category | flops | bytes accessed | tf_op | source)
XLA Modules:
  0.0 311.7 jit_solution(12788335768457517483)
XLA Ops:
  7.3 0.7 all-gather.2.cloned.1.call-update
  8.0 4.1 %copy.26 = bf16[2432,3,128]{0,2,1:T(8,128)(2,1)} copy(bf16[2432,3,128]{2,0,1:T(8,128)(2,1)} %param.18) | data formatting | bytes 3735552 | tf_op args[4]
  13.2 0.7 add_reduce_fusion
  13.9 34.3 %all-gather.2.cloned.1.call-done = bf16[1,16,16,2432]{3,2,0,1:T(8,128)(2,1)} async-done(((bf16[1,1,16,2432]{3,2,0,1:T(8,128)(2,1)}), bf16[1,16,16,2432]{3,2,0,1:T(8,128)(2,1)}) %all-gather.2.cloned.1.call-update) | async-done | bytes 1245200 | tf_op jit(solution)/shard_map/all_gather | solution.py:59
  48.2 1.7 convert_reduce_fusion
  49.9 1.7 multiply_reduce_fusion.1
  51.7 0.6 add_convert_fusion.1
  52.3 0.7 fusion.55
  53.8 12.6 %all_gather.10 = bf16[1024,128]{0,1:T(8,128)(2,1)S(1)} all-gather(bf16[256,128]{0,1:T(8,128)(2,1)S(1)} %fusion.35), channel_id=1, replica_groups=mesh['row'=16,'col'=4,'item'=4] {'col'}, dimensions={0}, use_global_device_ids=true | all-gather | bytes 327680 | tf_op jit(solution)/shard_map/all_gather | solution.py:114
  66.4 0.9 reshape.190
  67.3 1.0 copy.29
  68.3 13.0 %all_gather.11 = bf16[1024,128]{0,1:T(8,128)(2,1)} all-gather(bf16[256,128]{0,1:T(8,128)(2,1)S(1)} %bitcast.82), channel_id=1, replica_groups=mesh['row'=16,'col'=4,'item'=4] {'col'}, dimensions={0}, use_global_device_ids=true | all-gather | bytes 327680 | tf_op jit(solution)/shard_map/all_gather | solution.py:115
  81.3 1.8 reshape.191
  83.1 1.7 copy.30
  84.8 6.1 %while.14 = (s32[]{:T(128)}, f32[2,256]{1,0:T(2,128)S(1)}, f32[2,256]{1,0:T(2,128)S(1)}, f32[2,256,64]{1,2,0:T(8,128)S(1)}, bf16[4,256,2,64]{1,3,2,0:T(8,128)(2,...) while((s32[]{:T(128)}, f32[2,256]{1,0:T(2,128)S(1)}, ...), condition=%wide.region_9.10_spmd, body=%wide.region_6.9_spmd.sunk | while | flops 34407424 | bytes 2064985 | solution.py:119
  85.2 1.1 convolution_add_fusion.2
  86.8 1.1 convolution_add_fusion.2
  88.3 1.1 convolution_add_fusion.2
  89.8 1.1 convolution_add_fusion.2
  91.0 2.7 convolution_convert_fusion
  93.7 124.3 %all-reduce.2.cloned.1.call-done = bf16[256,2432]{1,0:T(8,128)(2,1)} async-done(((bf16[256,2432]{1,0:T(8,128)(2,1)}), bf16[256,2432]{1,0:T(8,128)(2,1)}) %all-reduce.2.cloned.1.call-update) | async-done | bytes 1245200 | tf_op jit(solution)/shard_map/psum | solution.py:129
  218.0 2.2 fusion.51
  220.2 1.4 copy-done.2
  221.6 0.4 multiply_reduce_fusion
  222.0 7.5 %convolution_convert_fusion.1 = bf16[256,2432]{1,0:T(8,128)(2,1)} fusion(bf16[608,2432]{1,0:T(8,128)(2,1)S(1)} %copy-done, bf16[2432,608]{0,1:T(8,128)(2,1)} %param.21, f32[256,2432]{1,0:T(8,128)} %copy-done.2, f32[2432]{0:T(1024)S(1)} %get-tuple-element.58, f32[2432]{0:T(1024)S(1)} %copy-done.7, f32[256]{0:T(256)S(1)} %add_rsqrt_fusion.3, ...), kind=kOutput, calls=%fused_computation.16 | convolution fusion | flops 1519280128 | bytes 9671680 | tf_op jit(solution)/shard_map/dot_general | solution.py:140
  229.6 66.3 %reduce-scatter.2.cloned.1.call-done = bf16[16,2432]{1,0:T(8,128)(2,1)} async-done(((bf16[256,2432]{1,0:T(8,128)(2,1)}), bf16[16,2432]{1,0:T(8,128)(2,1)}) %reduce-scatter.2.cloned.1.call-update) | async-done | bytes 77840 | tf_op jit(solution)/shard_map/reduce_scatter | solution.py:139
  295.9 1.1 fusion.49
  297.0 1.7 multiply_reduce_fusion.2
  298.7 1.2 fusion.36
  300.0 2.6 collective-permute-start
  303.3 1.2 collective-permute-done
  304.6 0.6 multiply_add_fusion.2
  (69 shorter events, 3.2 us)
Async XLA Ops:
  7.2 214.8 %copy-start = (bf16[608,2432]{1,0:T(8,128)(2,1)S(1)}, bf16[608,2432]{1,0:T(8,128)(2,1)}, u32[]{:S(2)}) copy-start(bf16[608,2432]{1,0:T(8,128)(2,1)} %param.22) | copy-start | bytes 8871940
  7.2 4.9 %copy-start.4 = (bf16[1,154,2,128]{3,2,1,0:T(2,128)(2,1)S(1)}, bf16[1,154,2,128]{3,2,1,0:T(2,128)(2,1)}, u32[]{:S(2)}) copy-start(bf16[1,154,2,128]{3,2,1,0:T(2,128)(2,1)} %param.15) | copy-start | bytes 236548
  7.2 5.9 %copy-start.9 = (f32[2,64]{1,0:T(2,128)S(1)}, f32[2,64]{1,0:T(2,128)}, u32[]{:S(2)}) copy-start(f32[2,64]{1,0:T(2,128)} %param.19) | copy-start | bytes 1540
  7.2 6.0 %copy-start.6 = (f32[1,8,2432]{2,1,0:T(8,128)S(1)}, f32[1,8,2432]{2,1,0:T(8,128)}, u32[]{:S(2)}) copy-start(f32[1,8,2432]{2,1,0:T(8,128)} %param.17) | copy-start | bytes 233476
  7.2 41.0 %all-gather.2.cloned.1.call-start = ((), (), s32[]{:S(2)}) async-start(), calls=%async_computation.1 | async-start | bytes 1323008 | tf_op jit(solution)/shard_map/all_gather | solution.py:59
  7.9 210.0 %all-reduce.2.cloned.1.call-start = ((), (), s32[]{:S(2)}) async-start(), calls=%async_computation.2 | async-start | bytes 2490368 | tf_op jit(solution)/shard_map/psum | solution.py:129
  48.2 3.5 %copy-start.1 = (bf16[1,16,16,2432]{3,2,0,1:T(8,128)(2,1)S(1)}, bf16[1,16,16,2432]{3,2,0,1:T(8,128)(2,1)}, u32[]{:S(2)}) copy-start(bf16[1,16,16,2432]{3,2,0,1:T(8,128)(2,1)} %all-gather.2.cloned.1.call-done) | copy-start | bytes 3735556
  48.2 4.1 %copy-start.3 = (bf16[2432,3,128]{0,2,1:T(8,128)(2,1)S(1)}, bf16[2432,3,128]{0,2,1:T(8,128)(2,1)}, u32[]{:S(2)}) copy-start(bf16[2432,3,128]{0,2,1:T(8,128)(2,1)} %copy.26) | copy-start | bytes 5603332
  93.6 202.3 %reduce-scatter.2.cloned.1.call-start = ((), (), s32[]{:S(2)}) async-start(), calls=%async_computation.3 | async-start | bytes 1323008 | tf_op jit(solution)/shard_map/reduce_scatter | solution.py:139
  220.1 1.4 copy-start.2
  220.2 1.9 copy-start.7
  222.0 76.7 %copy-start.5 = (bf16[2432,64]{0,1:T(8,128)(2,1)S(1)}, bf16[2432,64]{0,1:T(8,128)(2,1)}, u32[]{:S(2)}) copy-start(bf16[2432,64]{0,1:T(8,128)(2,1)} %param.23) | copy-start | bytes 933892
  229.5 75.0 %copy-start.8 = (f32[1,1,1024]{2,1,0:T(1,128)S(1)}, f32[1,1,1024]{2,1,0:T(1,128)}, u32[]{:S(2)}) copy-start(f32[1,1,1024]{2,1,0:T(1,128)} %param.25) | copy-start | bytes 12292
  300.0 4.5 %collective-permute-start = (f32[1,1,1024]{2,1,0:T(1,128)S(1)}, f32[1,1,1024]{2,1,0:T(1,128)S(1)}, u32[]{:S(2)}, u32[]{:S(2)}) collective-permute-start(f32[1,1,1024]{2,1,0:T(1,128)S(1)} %reshape.194), channel_id=1, source_target_pairs={{0,1},{1,0},{2,3},{3,2},{4,5},{5,4},{6,7},{7,6},{8,9},{9,8},{10,11... | collective-permute-start | bytes 12296 | tf_op jit(solution)/shard_map/ppermute | solution.py:17
Sparse Core Ops, SparseCore 0:
  9.9 38.2 all-gather.1
  93.8 124.1 all-reduce.1
  229.7 66.1 reduce-scatter.1
where the time goes:
time: 312 us
  waiting for transfers between devices  227 us (73%)
  blocking collectives  25.6 us (8%)
  matrix products  18 us (6%)
  between operations  15.4 us (5%)
  local copies, waits for them, and re-layouts  11.5 us (4%)
  other arithmetic  11.5 us (4%)
    psum x1, waiting for transfers between devices, on_device(): lax.psum(jnp.dot(attended, output_weight, preferred_element_type=jnp.floa...  124 us
    reduce_scatter x1, waiting for transfers between devices, on_device(): lax.psum_scatter(jnp.dot(hidden, down_weight, preferred_element_type=jnp....  66.3 us
    all_gather x1, waiting for transfers between devices, on_device(): stripe_tokens = lax.all_gather(tokens, 'row', axis=1, tiled=True)  34.3 us
    all_gather x1, blocking collectives, on_device(): value_piece = lax.all_gather(values_image, 'col', axis=0, tiled=True)  13 us
    all_gather x1, blocking collectives, on_device(): key_piece = lax.all_gather(keys_image, 'col', axis=0, tiled=True)  12.6 us
    dot_general x1, matrix products, on_device(): jnp.dot(hidden, down_weight, preferred_element_type=jnp.float32)  7.51 us
  transfers between devices with their start and end apart: 4, of which 4 were waited for; matrix products, arithmetic and copies ran while one was open for 2% of the time, Pallas kernels for 0%

commit v1 on v0

--- a/solution.py
+++ b/solution.py
@@ -52,6 +52,17 @@
     step_index,
     latent,
 ):
+
+    def _detail_groups(local_x, payload, axis_id):
+        oldest = jnp.split(
+            lax.all_gather(
+                jnp.concatenate([local_x, payload], axis=1), axis_name=axis_id, tiled=True, axis=0
+            ),
+            [local_x.shape[1]],
+            1,
+        )
+        return oldest
+
     tile_rows = tokens.shape[1] * tokens.shape[2]
     model_width = tokens.shape[3]
     mod_rows = modulation[0]
@@ -111,8 +122,7 @@
         )
         return ((new_max, new_mass, new_sum), None)
 
-    key_piece = lax.all_gather(keys_image, "col", axis=0, tiled=True)
-    value_piece = lax.all_gather(values_image, "col", axis=0, tiled=True)
+    key_piece, value_piece = _detail_groups(keys_image, values_image, "col")
     blocks = key_piece.shape[0] // stripe_rows
     key_blocks = key_piece.reshape(blocks, stripe_rows, local_heads, HD)
     value_blocks = value_piece.reshape(blocks, stripe_rows, local_heads, HD)

time: 312 us -> 301 us (0.965)
  blocking collectives: 25.6 us -> 13.5 us
    all_gather x2 -> x1, blocking collectives: 25.6 us -> 13.5 us  [_detail_groups(): lax.all_gather(jnp.concatenate([local_x, payload], axis=1), axis_name=axi...]
where the time goes in v1:
time: 301 us; the launch traced here: 300 us
  waiting for transfers between devices  228 us (76%)
  matrix products  18 us (6%)
  between operations  15.4 us (5%)
  blocking collectives  13.5 us (4%)
  local copies, waits for them, and re-layouts  12.2 us (4%)
  other arithmetic  11 us (4%)
    psum x1, waiting for transfers between devices, on_device(): lax.psum(jnp.dot(attended, output_weight, preferred_element_type=jnp.floa...  124 us
    reduce_scatter x1, waiting for transfers between devices, on_device(): lax.psum_scatter(jnp.dot(hidden, down_weight, preferred_element_type=jnp....  66.3 us
    all_gather x1, waiting for transfers between devices, on_device(): stripe_tokens = lax.all_gather(tokens, 'row', axis=1, tiled=True)  34.8 us
    all_gather x1, blocking collectives, _detail_groups(): lax.all_gather(jnp.concatenate([local_x, payload], axis=1), axis_name=axi...  13.5 us
    dot_general x1, matrix products, on_device(): jnp.dot(hidden, down_weight, preferred_element_type=jnp.float32)  7.51 us
  transfers between devices with their start and end apart: 4, of which 4 were waited for; matrix products, arithmetic and copies ran while one was open for 2% of the time, Pallas kernels for 0%

profile of v1, /device:TPU:8, one launch (start us, length us, event | category | flops | bytes accessed | tf_op | source)
XLA Modules:
  0.0 300.3 jit_solution(9170764886882312194)
XLA Ops:
  7.3 0.7 all-gather.2.cloned.1.call-update
  8.0 4.1 %copy.26 = bf16[2432,3,128]{0,2,1:T(8,128)(2,1)} copy(bf16[2432,3,128]{2,0,1:T(8,128)(2,1)} %param.18) | data formatting | bytes 3735552 | tf_op args[4]
  13.4 34.8 %all-gather.2.cloned.1.call-done = bf16[1,16,16,2432]{3,2,0,1:T(8,128)(2,1)} async-done(((bf16[1,1,16,2432]{3,2,0,1:T(8,128)(2,1)}), bf16[1,16,16,2432]{3,2,0,1:T(8,128)(2,1)}) %all-gather.2.cloned.1.call-update) | async-done | bytes 1245200 | tf_op jit(solution)/shard_map/all_gather | solution.py:70
  48.2 1.7 convert_reduce_fusion
  49.9 1.7 multiply_reduce_fusion.1
  51.7 0.6 add_convert_fusion.1
  52.3 0.7 fusion.56
  53.8 13.5 %all_gather.7 = bf16[1024,256]{0,1:T(8,128)(2,1)S(1)} all-gather(bf16[256,256]{0,1:T(8,128)(2,1)S(1)} %pad_maximum_fusion), channel_id=1, replica_groups=mesh['row'=16,'col'=4,'item'=4] {'col'}, dimensions={0}, use_global_device_ids=true | all-gather | bytes 655360 | tf_op jit(solution)/shard_map/all_gather | solution.py:58
  67.3 0.7 fusion.53
  68.0 0.9 reshape.190
  68.9 1.0 copy.29
  69.9 1.8 reshape.191
  71.7 1.7 copy.30
  73.4 6.1 %while.14 = (s32[]{:T(128)}, f32[2,256]{1,0:T(2,128)S(1)}, f32[2,256]{1,0:T(2,128)S(1)}, f32[2,256,64]{1,2,0:T(8,128)S(1)}, bf16[4,256,2,64]{1,3,2,0:T(8,128)(2,...) while((s32[]{:T(128)}, f32[2,256]{1,0:T(2,128)S(1)}, ...), condition=%wide.region_9.10_spmd, body=%wide.region_6.9_spmd.sunk | while | flops 34407424 | bytes 2064985 | solution.py:129
  73.8 1.1 convolution_add_fusion.2
  74.9 0.3 fusion.76
  75.3 1.1 convolution_add_fusion.2
  76.9 1.1 convolution_add_fusion.2
  78.4 1.1 convolution_add_fusion.2
  79.5 2.7 convolution_convert_fusion
  82.3 124.3 %all-reduce.2.cloned.1.call-done = bf16[256,2432]{1,0:T(8,128)(2,1)} async-done(((bf16[256,2432]{1,0:T(8,128)(2,1)}), bf16[256,2432]{1,0:T(8,128)(2,1)}) %all-reduce.2.cloned.1.call-update) | async-done | bytes 1245200 | tf_op jit(solution)/shard_map/psum | solution.py:139
  206.5 2.2 fusion.51
  208.7 1.4 copy-done.2
  210.1 0.4 multiply_reduce_fusion
  210.6 7.5 %convolution_convert_fusion.1 = bf16[256,2432]{1,0:T(8,128)(2,1)} fusion(bf16[608,2432]{1,0:T(8,128)(2,1)S(1)} %copy-done, bf16[2432,608]{0,1:T(8,128)(2,1)} %param.21, f32[256,2432]{1,0:T(8,128)} %copy-done.2, f32[2432]{0:T(1024)S(1)} %get-tuple-element.58, f32[2432]{0:T(1024)S(1)} %get-tuple-element.59, f32[256]{0:T(256)S(1)} %add_rsqrt_fusion.3, ...), kind=kOutput, calls=%fused_computation.16 | convolution fusion | flops 1519280128 | bytes 9671680 | tf_op jit(solution)/shard_map/dot_general | solution.py:150
  218.1 66.3 %reduce-scatter.2.cloned.1.call-done = bf16[16,2432]{1,0:T(8,128)(2,1)} async-done(((bf16[256,2432]{1,0:T(8,128)(2,1)}), bf16[16,2432]{1,0:T(8,128)(2,1)}) %reduce-scatter.2.cloned.1.call-update) | async-done | bytes 77840 | tf_op jit(solution)/shard_map/reduce_scatter | solution.py:149
  284.5 1.1 fusion.49
  285.5 1.7 multiply_reduce_fusion.2
  287.3 1.2 fusion.36
  288.6 2.4 collective-permute-start
  291.7 1.4 collective-permute-done
  293.1 0.6 multiply_add_fusion.2
  (68 shorter events, 3.1 us)
Async XLA Ops:
  7.2 203.4 %copy-start = (bf16[608,2432]{1,0:T(8,128)(2,1)S(1)}, bf16[608,2432]{1,0:T(8,128)(2,1)}, u32[]{:S(2)}) copy-start(bf16[608,2432]{1,0:T(8,128)(2,1)} %param.22) | copy-start | bytes 8871940
  7.2 4.9 %copy-start.4 = (bf16[1,154,2,128]{3,2,1,0:T(2,128)(2,1)S(1)}, bf16[1,154,2,128]{3,2,1,0:T(2,128)(2,1)}, u32[]{:S(2)}) copy-start(bf16[1,154,2,128]{3,2,1,0:T(2,128)(2,1)} %param.15) | copy-start | bytes 236548
  7.2 5.9 %copy-start.8 = (f32[2,64]{1,0:T(2,128)S(1)}, f32[2,64]{1,0:T(2,128)}, u32[]{:S(2)}) copy-start(f32[2,64]{1,0:T(2,128)} %param.19) | copy-start | bytes 1540
  7.2 6.0 %copy-start.6 = (f32[1,8,2432]{2,1,0:T(8,128)S(1)}, f32[1,8,2432]{2,1,0:T(8,128)}, u32[]{:S(2)}) copy-start(f32[1,8,2432]{2,1,0:T(8,128)} %param.17) | copy-start | bytes 233476
  7.2 41.0 %all-gather.2.cloned.1.call-start = ((), (), s32[]{:S(2)}) async-start(), calls=%async_computation.1 | async-start | bytes 1323008 | tf_op jit(solution)/shard_map/all_gather | solution.py:70
  7.9 198.6 %all-reduce.2.cloned.1.call-start = ((), (), s32[]{:S(2)}) async-start(), calls=%async_computation.2 | async-start | bytes 2490368 | tf_op jit(solution)/shard_map/psum | solution.py:139
  48.2 3.5 %copy-start.1 = (bf16[1,16,16,2432]{3,2,0,1:T(8,128)(2,1)S(1)}, bf16[1,16,16,2432]{3,2,0,1:T(8,128)(2,1)}, u32[]{:S(2)}) copy-start(bf16[1,16,16,2432]{3,2,0,1:T(8,128)(2,1)} %all-gather.2.cloned.1.call-done) | copy-start | bytes 3735556
  48.2 4.1 %copy-start.3 = (bf16[2432,3,128]{0,2,1:T(8,128)(2,1)S(1)}, bf16[2432,3,128]{0,2,1:T(8,128)(2,1)}, u32[]{:S(2)}) copy-start(bf16[2432,3,128]{0,2,1:T(8,128)(2,1)} %copy.26) | copy-start | bytes 5603332
  82.2 202.2 %reduce-scatter.2.cloned.1.call-start = ((), (), s32[]{:S(2)}) async-start(), calls=%async_computation.3 | async-start | bytes 1323008 | tf_op jit(solution)/shard_map/reduce_scatter | solution.py:149
  208.7 1.4 copy-start.2
  210.6 76.7 %copy-start.5 = (bf16[2432,64]{0,1:T(8,128)(2,1)S(1)}, bf16[2432,64]{0,1:T(8,128)(2,1)}, u32[]{:S(2)}) copy-start(bf16[2432,64]{0,1:T(8,128)(2,1)} %param.23) | copy-start | bytes 933892
  218.1 75.0 %copy-start.7 = (f32[1,1,1024]{2,1,0:T(1,128)S(1)}, f32[1,1,1024]{2,1,0:T(1,128)}, u32[]{:S(2)}) copy-start(f32[1,1,1024]{2,1,0:T(1,128)} %param.25) | copy-start | bytes 12292
  288.6 4.5 %collective-permute-start = (f32[1,1,1024]{2,1,0:T(1,128)S(1)}, f32[1,1,1024]{2,1,0:T(1,128)S(1)}, u32[]{:S(2)}, u32[]{:S(2)}) collective-permute-start(f32[1,1,1024]{2,1,0:T(1,128)S(1)} %reshape.194), channel_id=1, source_target_pairs={{0,1},{1,0},{2,3},{3,2},{4,5},{5,4},{6,7},{7,6},{8,9},{9,8},{10,11... | collective-permute-start | bytes 12296 | tf_op jit(solution)/shard_map/ppermute | solution.py:17
Sparse Core Ops, SparseCore 0:
  9.9 38.2 all-gather.1
  82.3 124.1 all-reduce.1
  218.2 66.1 reduce-scatter.1
